TPU v7x, 512 devices: a whole 4x8x8 slice. The times are simulated.
512 devices in a mesh: grp: 16 (over z, core), sub: 32 (over y, x).
Axes of the slice: x: 4, y: 8, z: 8, core: 2. Of those that a mesh axis runs over, the one named last changes fastest.
Arguments:
- right_side: float32 [8192, 512], P(('grp', 'sub')), may hold values from -8 to 8
- metric: float32 [8192, 1536], P(('grp', 'sub')), may hold values from 0.3 to 3
- helmholtz: float32 [8192, 512], P(('grp', 'sub')), may hold values from 0.5 to 2
- jacobi: float32 [8192, 512], P(('grp', 'sub')), may hold values from 0.05 to 0.5
- pair_list: int32 [2, 524288], P(None, ('grp', 'sub')), may hold values from 0 to 8191
- shared_slots: int32 [512, 32, 128], P(('grp', 'sub')), may hold values from 0 to 8192, as said below
- face_points: int32 [2, 262144], P(None, ('grp', 'sub')), may hold values from 0 to 8191
- coarse_map: int32 [8, 8192], P(None, ('grp', 'sub')), may hold values from 0 to 63
- coarse_inverse: float32 [16, 64, 64], P('grp'), as said below
Outputs:
- solution: float32 [8192, 512], P(('grp', 'sub'))
- residual: float32 [8192, 512], P(('grp', 'sub'))
Inputs may be any that keep to these rules, and one draw needn't show every extreme that they name: `shared_slots`: entries equal to 8192 mark empty slots; the slot of device a for peer b in one group is filled exactly when the slot of b for a at the same position is; a device's slots for itself are empty; filled slots come first in each row. `coarse_inverse`: each group's matrix is symmetric and positive definite.
All inputs are finite; a program needn't handle non-finite values.
Results may differ from a plain program's by a relative error of at most 0.0003.
Values sent between devices are 32-bit elements; how exact they have to be, the bound alone decides.
A program may use at most 64 MiB of HBM per device.

v0:
```python
import jax
import jax.numpy as jnp
import numpy as np
from jax import lax
from jax.sharding import PartitionSpec as P

ITERS = 2
NC = 64


def extended(cells, sides, width):
    for axis, dim in sides:
        count = lax.axis_size(axis)
        ends = count - 1
        head = lax.slice_in_dim(cells, 0, width, axis=dim)
        tail = lax.slice_in_dim(cells, cells.shape[dim] - width, cells.shape[dim], axis=dim)
        cells = jnp.concatenate(
            [
                lax.ppermute(tail, axis, [(i, (i + 1) % count) for i in range(ends)]),
                cells,
                lax.ppermute(head, axis, [((i + 1) % count, i) for i in range(ends)]),
            ],
            axis=dim,
        )
    return cells


def tables():
    order_index = np.arange(8)
    colloc = np.cos(np.pi * order_index / 7.0)
    end_weights = (
        np.where((order_index == 0) | (order_index == 7), 2.0, 1.0) * (-1.0) ** order_index
    )
    spacing = colloc[:, None] - colloc[None, :] + np.eye(8)
    raw_matrix = np.outer(end_weights, 1.0 / end_weights) / spacing
    off_part = raw_matrix * (1.0 - np.eye(8))
    derivative = 0.25 * (off_part - np.eye(8) * off_part.sum(axis=1)[:, None])
    along_first = np.kron(derivative, np.eye(64)).T
    along_inner = np.concatenate(
        [np.kron(derivative, np.eye(8)).T, np.kron(np.eye(8), derivative).T], axis=1
    )
    point_index = np.arange(512)
    corner_index = np.arange(8)
    sign_first = 1.0 - 2.0 * (corner_index >> 2 & 1)
    sign_second = 1.0 - 2.0 * (corner_index >> 1 & 1)
    sign_third = 1.0 - 2.0 * (corner_index & 1)
    node_first = colloc[point_index // 64][:, None]
    node_second = colloc[point_index // 8 % 8][:, None]
    node_third = colloc[point_index % 8][:, None]
    corner = (
        0.5
        * (1.0 + sign_first[None, :] * node_first)
        * (0.5 * (1.0 + sign_second[None, :] * node_second))
        * (0.5 * (1.0 + sign_third[None, :] * node_third))
    )
    return (
        jnp.asarray(along_first, jnp.float32),
        jnp.asarray(along_inner, jnp.float32),
        jnp.asarray(corner, jnp.float32),
    )


def residual_product(resid, smoothed):
    return lax.psum(jnp.sum(resid * smoothed), ("grp", "sub"))


def body(
    right_side,
    metric,
    helmholtz,
    jacobi,
    pair_list,
    shared_slots,
    face_points,
    coarse_map,
    coarse_inverse,
):
    highest = lax.Precision.HIGHEST
    along_first, along_inner, corner = tables()
    elements = right_side.shape[0]
    points = elements * right_side.shape[1]
    slots = shared_slots[0]

    def assemble(field):
        flat = field.reshape(-1)
        total = (
            flat.at[pair_list[0]].add(flat[pair_list[1]]).at[pair_list[1]].add(flat[pair_list[0]])
        )
        padded = jnp.concatenate([flat, jnp.zeros((1,), jnp.float32)])
        sent = padded[slots]
        received = lax.all_to_all(sent, "sub", split_axis=0, concat_axis=0, tiled=True)
        total = (
            jnp.concatenate([total, jnp.zeros((1,), jnp.float32)]).at[slots].add(received)[:points]
        )
        face_values = flat[face_points]
        rim = extended(face_values, (("grp", 0),), 1)
        total = total.at[face_points[0]].add(rim[0]).at[face_points[1]].add(rim[3])
        return total.reshape(field.shape)

    onehot = (coarse_map.reshape(-1)[:, None] == jnp.arange(NC, dtype=jnp.int32)[None, :]).astype(
        jnp.float32
    )

    def precondition(resid):
        vertex = jnp.dot(resid, corner, precision=highest)
        partial_coarse = jnp.dot(vertex.T.reshape(-1), onehot, precision=highest)
        coarse = lax.psum(partial_coarse, "sub")
        solved = jnp.dot(coarse_inverse[0], coarse, precision=highest)
        at_vertex = jnp.dot(onehot, solved, precision=highest).reshape(8, -1)
        return jacobi * resid + jnp.dot(at_vertex.T, corner.T, precision=highest)

    solution = jnp.zeros_like(right_side)
    residual = right_side
    smoothed = precondition(residual)
    direction = smoothed
    rz_now = residual_product(residual, smoothed)
    for iteration in range(ITERS):
        summed = assemble(direction)
        grad_first = jnp.dot(summed, along_first, precision=highest)
        inner = jnp.dot(summed.reshape(elements * 8, 64), along_inner, precision=highest)
        grad_second = inner[:, :64].reshape(elements, 512)
        grad_third = inner[:, 64:].reshape(elements, 512)
        flux_first = metric[:, :512] * grad_first
        flux_second = (metric[:, 512:1024] * grad_second).reshape(elements * 8, 64)
        flux_third = (metric[:, 1024:] * grad_third).reshape(elements * 8, 64)
        back = jnp.dot(flux_first, along_first.T, precision=highest)
        fluxes = jnp.concatenate([flux_second, flux_third], axis=1)
        back = back + jnp.dot(fluxes, along_inner.T, precision=highest).reshape(elements, 512)
        image = assemble(back) + helmholtz * direction
        alpha = rz_now / lax.psum(jnp.sum(direction * image), ("grp", "sub"))
        solution = solution + alpha * direction
        residual = residual - alpha * image
        if iteration + 1 < ITERS:
            smoothed = precondition(residual)
            rz_new = residual_product(residual, smoothed)
            direction = smoothed + rz_new / rz_now * direction
            rz_now = rz_new
    return (solution, residual)


def solution(mesh):
    in_specs = (
        P(("grp", "sub"), None),
        P(("grp", "sub"), None),
        P(("grp", "sub"), None),
        P(("grp", "sub"), None),
        P(None, ("grp", "sub")),
        P(("grp", "sub"), None, None),
        P(None, ("grp", "sub")),
        P(None, ("grp", "sub")),
        P("grp", None, None),
    )
    out_specs = (P(("grp", "sub"), None), P(("grp", "sub"), None))
    return jax.shard_map(body, mesh=mesh, in_specs=in_specs, out_specs=out_specs, check_vma=False)
```

profile of v0, /device:TPU:1, one launch (start us, length us, event | category | flops | bytes accessed | tf_op | source)
XLA Modules:
  0.0 937.1 jit_solution(3076881587278794797)
XLA Ops:
  3.3 61.9 %psum.42 = f32[64]{0:T(128)S(1)} all-reduce(f32[64]{0:T(128)S(1)} %convolution_bitcast_fusion.5), channel_id=1, replica_groups=mesh['grp'=16,'sub'=32] {'sub'}, use_global_device_ids=true, to_apply=%region_0.0 | all-reduce | flops 64 | bytes 512 | tf_op jit(solution)/shard_map/psum | solution.py:107
  67.3 40.6 %gather_fusion.2 = f32[4096]{0:T(1024)} fusion(f32[8193]{0:T(1024)S(1)} %pad_maximum_fusion.6, s32[4096]{0:T(1024)S(1)} %broadcast_clamp_fusion), kind=kCustom, calls=%fused_computation.2 | custom fusion | bytes 49152 | tf_op jit(solution)/shard_map/gather | solution.py:90
  107.8 4.3 all-to-all-start
  112.2 6.2 gather_fusion.3
  118.4 19.0 %collective-permute-start = (f32[1,512]{1,0:T(1,128)S(1)}, f32[1,512]{1,0:T(1,128)S(1)}, u32[]{:S(2)}, u32[]{:S(2)}) collective-permute-start(f32[1,512]{1,0:T(1,128)S(1)} %bitcast.169), channel_id=1, source_target_pairs={{0,32},{32,64},{64,96},{96,128},{128,160},{160,192},{192,224},{224... | collective-permute-start | bytes 6152 | tf_op jit(solution)/shard_map/ppermute | solution.py:19
  139.4 6.2 gather_fusion
  145.6 6.2 gather_fusion.1
  151.7 6.1 scatter_fusion
  157.9 6.1 scatter_fusion.1
  164.0 26.2 %scatter_fusion.2 = f32[8193]{0:T(1024)S(1)} fusion(f32[8193]{0:T(1024)S(1)} %pad_maximum_fusion.7, s32[4096]{0:T(1024)S(1)} %fusion.8, f32[4096]{0:T(1024)S(1)} %bitcast.146), kind=kCustom, calls=%fused_computation.18 | custom fusion | flops 4096 | bytes 65536 | tf_op jit(solution)/shard_map/scatter-add | solution.py:93
  190.3 3.4 scatter_fusion.3
  193.7 3.6 scatter_fusion.4
  201.7 6.2 gather_fusion.4
  207.9 6.2 gather_fusion.5
  214.0 6.2 gather_fusion.7
  220.2 40.6 %gather_fusion.6 = f32[4096]{0:T(1024)} fusion(f32[8193]{0:T(1024)S(1)} %pad_maximum_fusion.4, s32[4096]{0:T(1024)S(1)} %broadcast_clamp_fusion), kind=kCustom, calls=%fused_computation.6 | custom fusion | bytes 49152 | tf_op jit(solution)/shard_map/gather | solution.py:90
  260.8 6.1 scatter_fusion.5
  266.9 6.1 scatter_fusion.6
  273.0 8.5 all-to-all-start.1
  281.5 4.2 collective-permute-start.2
  290.0 26.2 %scatter_fusion.7 = f32[8193]{0:T(1024)S(1)} fusion(f32[8193]{0:T(1024)S(1)} %pad_maximum_fusion.5, s32[4096]{0:T(1024)S(1)} %fusion.8, f32[4096]{0:T(1024)S(1)} %bitcast.148), kind=kCustom, calls=%fused_computation.23 | custom fusion | flops 4096 | bytes 65536 | tf_op jit(solution)/shard_map/scatter-add | solution.py:93
  316.3 3.4 scatter_fusion.8
  319.7 3.4 scatter_fusion.9
  324.5 101.9 %all-reduce = (f32[]{:T(128)}, f32[]{:T(128)}) all-reduce(f32[]{:T(128)} %get-tuple-element.3, f32[]{:T(128)} %get-tuple-element.2), channel_id=1, replica_groups=mesh['grp'=16,'sub'=32] {'grp','sub'}, use_global_device_ids=true, to_apply=%region_2.0 | all-reduce | flops 2 | bytes 16 | tf_op jit(solution)/shard_map/psum | solution.py:64
  428.5 57.5 %psum.45 = f32[64]{0:T(128)S(1)} all-reduce(f32[64]{0:T(128)S(1)} %convolution_bitcast_fusion.2), channel_id=1, replica_groups=mesh['grp'=16,'sub'=32] {'sub'}, use_global_device_ids=true, to_apply=%region_15.0 | all-reduce | flops 64 | bytes 512 | tf_op jit(solution)/shard_map/psum | solution.py:107
  487.5 107.9 %psum.46 = f32[]{:T(128)} all-reduce(f32[]{:T(128)} %get-tuple-element.28), channel_id=1, replica_groups=mesh['grp'=16,'sub'=32] {'grp','sub'}, use_global_device_ids=true, to_apply=%region_17.0 | all-reduce | flops 1 | bytes 8 | tf_op jit(solution)/shard_map/psum | solution.py:64
  596.9 6.2 gather_fusion.8
  603.0 6.2 gather_fusion.9
  609.2 6.2 gather_fusion.11
  615.4 40.6 %gather_fusion.10 = f32[4096]{0:T(1024)} fusion(f32[8193]{0:T(1024)S(1)} %pad_maximum_fusion.2, s32[4096]{0:T(1024)S(1)} %broadcast_clamp_fusion), kind=kCustom, calls=%fused_computation.10 | custom fusion | bytes 49152 | tf_op jit(solution)/shard_map/gather | solution.py:90
  655.9 6.1 scatter_fusion.10
  662.0 6.1 scatter_fusion.11
  668.1 6.0 all-to-all-start.2
  674.2 3.6 collective-permute-start.4
  682.7 26.2 %scatter_fusion.12 = f32[8193]{0:T(1024)S(1)} fusion(f32[8193]{0:T(1024)S(1)} %pad_maximum_fusion.3, s32[4096]{0:T(1024)S(1)} %fusion.8, f32[4096]{0:T(1024)S(1)} %bitcast.149), kind=kCustom, calls=%fused_computation.28 | custom fusion | flops 4096 | bytes 65536 | tf_op jit(solution)/shard_map/scatter-add | solution.py:93
  709.0 3.4 scatter_fusion.13
  712.4 3.6 scatter_fusion.14
  719.2 6.2 gather_fusion.12
  725.4 6.2 gather_fusion.13
  731.6 6.2 gather_fusion.15
  737.7 40.6 %gather_fusion.14 = f32[4096]{0:T(1024)} fusion(f32[8193]{0:T(1024)S(1)} %pad_maximum_fusion, s32[4096]{0:T(1024)S(1)} %broadcast_clamp_fusion), kind=kCustom, calls=%fused_computation.14 | custom fusion | bytes 49152 | tf_op jit(solution)/shard_map/gather | solution.py:90
  778.3 6.1 scatter_fusion.15
  784.4 6.1 scatter_fusion.16
  790.5 5.6 all-to-all-start.3
  796.1 4.2 collective-permute-start.6
  804.6 26.2 %scatter_fusion.17 = f32[8193]{0:T(1024)S(1)} fusion(f32[8193]{0:T(1024)S(1)} %pad_maximum_fusion.1, s32[4096]{0:T(1024)S(1)} %fusion.8, f32[4096]{0:T(1024)S(1)} %bitcast.147), kind=kCustom, calls=%fused_computation.33 | custom fusion | flops 4096 | bytes 65536 | tf_op jit(solution)/shard_map/scatter-add | solution.py:93
  830.9 3.4 scatter_fusion.18
  838.3 96.4 %psum.47 = f32[]{:T(128)} all-reduce(f32[]{:T(128)} %multiply_reduce_fusion), channel_id=1, replica_groups=mesh['grp'=16,'sub'=32] {'grp','sub'}, use_global_device_ids=true, to_apply=%region_29.0 | all-reduce | flops 1 | bytes 8 | tf_op jit(solution)/shard_map/psum | solution.py:130
  (128 shorter events, 36.1 us)
Async XLA Ops:
  0.6 64.6 %copy-start = (f32[1,64,64]{2,1,0:T(8,128)S(1)}, f32[1,64,64]{2,1,0:T(8,128)}, u32[]{:S(2)}) copy-start(f32[1,64,64]{2,1,0:T(8,128)} %param.20) | copy-start | bytes 49156
  0.6 65.0 %copy-start.2 = (f32[512,8]{1,0:T(8,128)S(1)}, f32[512,8]{1,0:T(8,128)}, u32[]{:S(2)}) copy-start(f32[512,8]{1,0:T(8,128)} %constant.5.clone) | copy-start | bytes 49156
  65.3 0.8 copy-start.3
  65.3 0.8 copy-start.6
  66.5 0.7 copy-start.10
  107.8 4.3 copy-start.11
  107.8 56.2 %all-to-all-start = ((f32[32,1,128]{2,1,0:T(1,128)}), f32[32,1,128]{2,1,0:T(1,128)S(1)}, u32[]{:S(2)}, u32[]{:S(2)}) async-start(f32[32,1,128]{2,1,0:T(1,128)} %bitcast.12), calls=%async_computation | async-start | bytes 32768 | tf_op jit(solution)/shard_map/all_to_all | solution.py:91
  118.4 71.9 %collective-permute-start = (f32[1,512]{1,0:T(1,128)S(1)}, f32[1,512]{1,0:T(1,128)S(1)}, u32[]{:S(2)}, u32[]{:S(2)}) collective-permute-start(f32[1,512]{1,0:T(1,128)S(1)} %bitcast.169), channel_id=1, source_target_pairs={{0,32},{32,64},{64,96},{96,128},{128,160},{160,192},{192,224},{224... | collective-permute-start | bytes 6152 | tf_op jit(solution)/shard_map/ppermute | solution.py:19
  137.4 2.0 copy-start.12
  137.4 56.3 %collective-permute-start.1 = (f32[1,512]{1,0:T(1,128)S(1)}, f32[1,512]{1,0:T(1,128)S(1)}, u32[]{:S(2)}, u32[]{:S(2)}) collective-permute-start(f32[1,512]{1,0:T(1,128)S(1)} %bitcast.167), channel_id=1, source_target_pairs={{32,0},{64,32},{96,64},{128,96},{160,128},{192,160},{224,192},{256... | collective-permute-start | bytes 6152 | tf_op jit(solution)/shard_map/ppermute | solution.py:21
  193.7 3.7 copy-start.8
  193.7 4.4 copy-start.5
  197.3 2.8 copy-start.1
  198.1 0.8 copy-start.9
  198.9 0.8 copy-start.7
  273.0 17.1 %all-to-all-start.1 = ((f32[32,1,128]{2,1,0:T(1,128)}), f32[32,1,128]{2,1,0:T(1,128)S(1)}, u32[]{:S(2)}, u32[]{:S(2)}) async-start(f32[32,1,128]{2,1,0:T(1,128)} %bitcast.22), calls=%async_computation.1 | async-start | bytes 32768 | tf_op jit(solution)/shard_map/all_to_all | solution.py:91
  281.5 34.8 %collective-permute-start.2 = (f32[1,512]{1,0:T(1,128)S(1)}, f32[1,512]{1,0:T(1,128)S(1)}, u32[]{:S(2)}, u32[]{:S(2)}) collective-permute-start(f32[1,512]{1,0:T(1,128)S(1)} %bitcast.173), channel_id=1, source_target_pairs={{0,32},{32,64},{64,96},{96,128},{128,160},{160,192},{192,224},{224... | collective-permute-start | bytes 6152 | tf_op jit(solution)/shard_map/ppermute | solution.py:19
  285.7 34.0 %collective-permute-start.3 = (f32[1,512]{1,0:T(1,128)S(1)}, f32[1,512]{1,0:T(1,128)S(1)}, u32[]{:S(2)}, u32[]{:S(2)}) collective-permute-start(f32[1,512]{1,0:T(1,128)S(1)} %bitcast.170), channel_id=1, source_target_pairs={{32,0},{64,32},{96,64},{128,96},{160,128},{192,160},{224,192},{256... | collective-permute-start | bytes 6152 | tf_op jit(solution)/shard_map/ppermute | solution.py:21
  323.1 0.8 copy-start.4
  668.1 14.6 %all-to-all-start.2 = ((f32[32,1,128]{2,1,0:T(1,128)}), f32[32,1,128]{2,1,0:T(1,128)S(1)}, u32[]{:S(2)}, u32[]{:S(2)}) async-start(f32[32,1,128]{2,1,0:T(1,128)} %bitcast.33), calls=%async_computation.2 | async-start | bytes 32768 | tf_op jit(solution)/shard_map/all_to_all | solution.py:91
  674.2 34.8 %collective-permute-start.4 = (f32[1,512]{1,0:T(1,128)S(1)}, f32[1,512]{1,0:T(1,128)S(1)}, u32[]{:S(2)}, u32[]{:S(2)}) collective-permute-start(f32[1,512]{1,0:T(1,128)S(1)} %bitcast.174), channel_id=1, source_target_pairs={{0,32},{32,64},{64,96},{96,128},{128,160},{160,192},{192,224},{224... | collective-permute-start | bytes 6152 | tf_op jit(solution)/shard_map/ppermute | solution.py:19
  677.8 34.5 %collective-permute-start.5 = (f32[1,512]{1,0:T(1,128)S(1)}, f32[1,512]{1,0:T(1,128)S(1)}, u32[]{:S(2)}, u32[]{:S(2)}) collective-permute-start(f32[1,512]{1,0:T(1,128)S(1)} %bitcast.171), channel_id=1, source_target_pairs={{32,0},{64,32},{96,64},{128,96},{160,128},{192,160},{224,192},{256... | collective-permute-start | bytes 6152 | tf_op jit(solution)/shard_map/ppermute | solution.py:21
  790.5 14.1 %all-to-all-start.3 = ((f32[32,1,128]{2,1,0:T(1,128)}), f32[32,1,128]{2,1,0:T(1,128)S(1)}, u32[]{:S(2)}, u32[]{:S(2)}) async-start(f32[32,1,128]{2,1,0:T(1,128)} %bitcast.39), calls=%async_computation.3 | async-start | bytes 32768 | tf_op jit(solution)/shard_map/all_to_all | solution.py:91
  796.1 34.8 %collective-permute-start.6 = (f32[1,512]{1,0:T(1,128)S(1)}, f32[1,512]{1,0:T(1,128)S(1)}, u32[]{:S(2)}, u32[]{:S(2)}) collective-permute-start(f32[1,512]{1,0:T(1,128)S(1)} %bitcast.172), channel_id=1, source_target_pairs={{0,32},{32,64},{64,96},{96,128},{128,160},{160,192},{192,224},{224... | collective-permute-start | bytes 6152 | tf_op jit(solution)/shard_map/ppermute | solution.py:19
  800.3 34.0 %collective-permute-start.7 = (f32[1,512]{1,0:T(1,128)S(1)}, f32[1,512]{1,0:T(1,128)S(1)}, u32[]{:S(2)}, u32[]{:S(2)}) collective-permute-start(f32[1,512]{1,0:T(1,128)S(1)} %bitcast.168), channel_id=1, source_target_pairs={{32,0},{64,32},{96,64},{128,96},{160,128},{192,160},{224,192},{256... | collective-permute-start | bytes 6152 | tf_op jit(solution)/shard_map/ppermute | solution.py:21
where the time goes:
time: 945 us; the launch traced here: 937 us
  blocking collectives  426 us (45%)
  local copies, waits for them, and re-layouts  242 us (26%)
  other arithmetic  183 us (19%)
  starting transfers between devices  63.1 us (7%)
    psum x2, blocking collectives, residual_product(): return lax.psum(jnp.sum(resid * smoothed), ('grp', 'sub'))  210 us
    gather x4, local copies, waits for them, and re-layouts, assemble(): sent = padded[slots]  162 us
    psum x2, blocking collectives, precondition(): coarse = lax.psum(partial_coarse, 'sub')  119 us
    scatter-add x4, other arithmetic, assemble(): jnp.concatenate([total, jnp.zeros((1,), jnp.float32)]).at[slots]  105 us
    psum x1, blocking collectives, body(): alpha = rz_now / lax.psum(jnp.sum(direction * image), ('grp', 'sub'))  96.4 us
    scatter-add x8, other arithmetic, assemble(): flat.at[pair_list[0]].add(flat[pair_list[1]]).at[pair_list[1]]  48.8 us
    ppermute x4, starting transfers between devices, extended(): lax.ppermute(tail, axis, [(i, (i + 1) % count) for i in range(ends)])  31 us
    scatter-add x8, other arithmetic, assemble(): total = total.at[face_points[0]].add(rim[0]).at[face_points[1]].add(rim[3])  27.5 us
  transfers between devices with their start and end apart: 12, of which 3 were waited for; matrix products, arithmetic and copies ran while one was open for 16% of the time, Pallas kernels for 0%

commit v1 on v0

v1 whole, which is shorter than its diff:
```python
import functools

import jax
import jax.numpy as jnp
import numpy as np
from jax import lax
from jax.experimental import pallas as pl
from jax.experimental.pallas import tpu as pltpu
from jax.sharding import PartitionSpec as P

MESH = pl.DeviceIdType.MESH
F32 = jnp.float32
BF16 = jnp.bfloat16
PAIR = 8
FACE = 4


def tables():
    order_index = np.arange(8)
    colloc = np.cos(np.pi * order_index / 7.0)
    end_weights = (
        np.where((order_index == 0) | (order_index == 7), 2.0, 1.0) * (-1.0) ** order_index
    )
    spacing = colloc[:, None] - colloc[None, :] + np.eye(8)
    raw_matrix = np.outer(end_weights, 1.0 / end_weights) / spacing
    off_part = raw_matrix * (1.0 - np.eye(8))
    derivative = 0.25 * (off_part - np.eye(8) * off_part.sum(axis=1)[:, None])
    derivative = derivative.astype(np.float32).astype(np.float64)
    eye2, eye8, eye16 = np.eye(2), np.eye(8), np.eye(16)

    def rows_matrix(mat):
        def part(out_low, in_low):
            return np.kron(mat[out_low::2, in_low::2], eye16)

        return np.block([[part(0, 0), part(0, 1)], [part(1, 1), part(1, 0)]])

    along_second = np.kron(eye2, np.kron(derivative, eye8)).T
    along_third = np.kron(eye16, derivative).T
    stack = [
        along_second,
        along_third,
        along_second.T,
        along_third.T,
        rows_matrix(derivative),
        rows_matrix(derivative.T),
    ]
    high = [np.asarray(m, np.float32).astype(jnp.bfloat16) for m in stack]
    low = [
        (np.asarray(m, np.float32) - h.astype(np.float32)).astype(jnp.bfloat16)
        for m, h in zip(stack, high)
    ]
    mats = np.stack(high + low)
    point_index = np.arange(512)
    corner_index = np.arange(8)
    sign_first = 1.0 - 2.0 * (corner_index >> 2 & 1)
    sign_second = 1.0 - 2.0 * (corner_index >> 1 & 1)
    sign_third = 1.0 - 2.0 * (corner_index & 1)
    node_first = colloc[point_index // 64][:, None]
    node_second = colloc[point_index // 8 % 8][:, None]
    node_third = colloc[point_index % 8][:, None]
    corner = (
        0.5
        * (1.0 + sign_first[None, :] * node_first)
        * (0.5 * (1.0 + sign_second[None, :] * node_second))
        * (0.5 * (1.0 + sign_third[None, :] * node_third))
    )
    return jnp.asarray(mats), jnp.asarray(corner.T, F32)


def kernel(
    ns,
    ng,
    right_ref,
    metric_ref,
    helm_ref,
    jac_ref,
    pair_ref,
    slots_ref,
    face_ref,
    map_ref,
    cinv_ref,
    mats_ref,
    corner_ref,
    sol_ref,
    res_ref,
    idx,
    hi_ref,
    lo_ref,
    ohlo,
    x_ref,
    val_ref,
    cscr,
    mcol,
    send_s,
    recv_s,
    send_f,
    recv_f,
    send_r,
    recv_r,
    send_b,
    recv_b,
    send_sem,
    recv_sem,
):
    g = lax.axis_index("grp")
    s = lax.axis_index("sub")
    nxt, prv = lax.rem(g + 1, ng), lax.rem(g + ng - 1, ng)
    rows = 2 * PAIR + ns + 2 * FACE
    tiles = rows // 8
    at_face = 2 * PAIR + ns

    recv_s[...] = jnp.zeros_like(recv_s)

    barrier = pltpu.get_barrier_semaphore()

    def greet_sub(k, carry):
        pl.semaphore_signal(
            barrier, inc=1, device_id={"sub": lax.rem(s + k, ns)}, device_id_type=MESH
        )
        return carry

    def greet_grp(k, carry):
        pl.semaphore_signal(
            barrier, inc=1, device_id={"grp": lax.rem(g + k, ng)}, device_id_type=MESH
        )
        return carry

    lax.fori_loop(1, ns, greet_sub, 0)
    lax.fori_loop(1, ng, greet_grp, 0)

    def cube(ref, base=0):
        return jnp.concatenate(
            [ref[:, base + 128 * k : base + 128 * (k + 1)] for k in range(4)], axis=0
        )

    def total(x):
        return jnp.sum(jnp.sum(x, axis=0, keepdims=True), axis=1, keepdims=True)

    lane = lax.broadcasted_iota(jnp.int32, (1, 128), 1)

    def pick(row, k):
        return jnp.sum(jnp.where(lane == k, row, 0.0), axis=1, keepdims=True)

    def put(k, value):
        return jnp.where(lane == k, value, 0.0)

    eye_16 = lax.broadcasted_iota(jnp.int32, (16, 16), 0) == lax.broadcasted_iota(
        jnp.int32, (16, 16), 1
    )
    lane_16 = lax.broadcasted_iota(jnp.int32, (16, 128), 1).astype(F32)
    for q in range(8):
        column = jnp.sum(
            jnp.where(eye_16, map_ref[q : q + 1, :].astype(F32), 0.0), axis=1, keepdims=True
        )
        mcol[q] = jnp.where(lane_16 == column, 1.0, 0.0)
    cscr[...] = jnp.zeros_like(cscr)
    cscr[:, :64] = cinv_ref[0]

    def restrict(x):
        row = jnp.zeros((1, 128), F32)
        for q in range(8):
            acc = x[:16] * corner_ref[q : q + 1, :128]
            for k in range(1, 4):
                acc += x[16 * k : 16 * (k + 1)] * corner_ref[q : q + 1, 128 * k : 128 * (k + 1)]
            vertex = jnp.sum(acc, axis=1, keepdims=True)
            row += jnp.sum(vertex * mcol[q], axis=0, keepdims=True)
        return row

    eye_64 = lax.broadcasted_iota(jnp.int32, (64, 128), 0) == lax.broadcasted_iota(
        jnp.int32, (64, 128), 1
    )

    def prolong(coarse):
        column = jnp.sum(jnp.where(eye_64, coarse, 0.0), axis=1, keepdims=True)
        solved = jnp.sum(cscr[...] * column, axis=0, keepdims=True)
        blocks = [jnp.zeros((16, 128), F32) for _ in range(4)]
        for q in range(8):
            at_vertex = jnp.sum(mcol[q] * solved, axis=1, keepdims=True)
            for k in range(4):
                blocks[k] += at_vertex * corner_ref[q : q + 1, 128 * k : 128 * (k + 1)]
        return jnp.concatenate(blocks, axis=0)

    def copy_sub(src, dst, sem, peer):
        return pltpu.make_async_remote_copy(
            src_ref=src,
            dst_ref=dst,
            send_sem=send_sem.at[sem],
            recv_sem=recv_sem.at[sem],
            device_id={"sub": peer},
            device_id_type=MESH,
        )

    def copy_grp(src, dst, sem, peer):
        return pltpu.make_async_remote_copy(
            src_ref=src,
            dst_ref=dst,
            send_sem=send_sem.at[sem],
            recv_sem=recv_sem.at[sem],
            device_id={"grp": peer},
            device_id_type=MESH,
        )

    def wait_bytes(ref, sem):
        pltpu.make_async_copy(ref, ref, sem).wait()

    def reduce_sub(phase, row):
        send_r[phase] = row
        recv_r[phase, s] = row

        def go(k, carry):
            peer = lax.rem(s + k, ns)
            copy_sub(send_r.at[phase], recv_r.at[phase, s], 12 + phase, peer).start()
            return carry

        lax.fori_loop(1, ns, go, 0)
        wait_bytes(recv_r.at[phase, pl.ds(0, ns - 1)], recv_sem.at[12 + phase])
        return jnp.sum(recv_r[phase], axis=0)

    def reduce_grp(phase, row):
        send_b[phase] = row
        recv_b[phase, g] = row

        def go(k, carry):
            peer = lax.rem(g + k, ng)
            copy_grp(send_b.at[phase], recv_b.at[phase, g], 15 + phase, peer).start()
            return carry

        lax.fori_loop(1, ng, go, 0)
        wait_bytes(recv_b.at[phase, pl.ds(0, ng - 1)], recv_sem.at[15 + phase])
        return jnp.sum(recv_b[phase], axis=0)

    residual = cube(right_ref)
    partial_coarse = restrict(residual)

    for k in range(PAIR):
        idx[k : k + 1, :] = pair_ref[0:1, 128 * k : 128 * (k + 1)]
        idx[PAIR + k : PAIR + k + 1, :] = pair_ref[1:2, 128 * k : 128 * (k + 1)]
    idx[2 * PAIR : at_face, :] = slots_ref[0]
    for k in range(FACE):
        idx[at_face + k : at_face + k + 1, :] = face_ref[0:1, 128 * k : 128 * (k + 1)]
        idx[at_face + FACE + k : at_face + FACE + k + 1, :] = face_ref[
            1:2, 128 * k : 128 * (k + 1)
        ]
    points = idx[...]
    row_of = ((points >> 7) & 3) * 16 + (points >> 9)
    hi_ref[...] = jnp.where(points >= 8192, 1024, row_of)
    lo_ref[...] = points & 127

    pl.semaphore_wait(barrier, ns + ng - 2)

    coarse = reduce_sub(0, partial_coarse)

    sub_128 = lax.broadcasted_iota(jnp.int32, (128, 128), 0)
    sub_64 = lax.broadcasted_iota(jnp.int32, (64, 128), 0)

    def build(t, carry):
        low = lo_ref[pl.ds(pl.multiple_of(t * 8, 8), 8), :]
        ohlo[t] = jnp.concatenate(
            [jnp.where(sub_128 == low[r : r + 1], 1.0, 0.0).astype(BF16) for r in range(8)],
            axis=1,
        )
        return carry

    lax.fori_loop(0, tiles, build, 0)

    def gather(x):
        x_ref[...] = x
        high = hi_ref[...]
        low = lo_ref[...]

        def step(t, acc):
            block = x_ref[pl.ds(pl.multiple_of(t * 8, 8), 8), :]
            for r in range(8):
                row = jnp.broadcast_to(block[r : r + 1], (rows, 128))
                got = jnp.take_along_axis(row, low, axis=1, mode="promise_in_bounds")
                acc = jnp.where(high == t * 8 + r, got, acc)
            return acc

        return lax.fori_loop(0, 8, step, jnp.zeros((rows, 128), F32))

    def scatter(first, last, acc):
        def step(t, acc):
            at = pl.ds(pl.multiple_of(t * 8, 8), 8)
            high = hi_ref[at, :]
            value = val_ref[at, :]
            upper = value.astype(BF16).astype(F32)
            lower = value - upper
            parts = []
            for r in range(8):
                hit = sub_64 == high[r : r + 1]
                parts.append(
                    jnp.concatenate(
                        [
                            jnp.where(hit, upper[r : r + 1], 0.0),
                            jnp.where(hit, lower[r : r + 1], 0.0),
                        ],
                        axis=0,
                    ).astype(BF16)
                )
            left = jnp.concatenate(parts, axis=1)
            return acc + lax.dot_general(
                left, ohlo[t], (((1,), (1,)), ((), ())), preferred_element_type=F32
            )

        return lax.fori_loop(first, last, step, acc)

    def assemble(phase, x):
        got = gather(x)
        send_s[phase] = got[2 * PAIR : at_face].reshape(ns, 1, 128)
        send_f[phase, 0] = got[at_face : at_face + FACE]
        send_f[phase, 1] = got[at_face + FACE :]

        def go(k, carry):
            peer = lax.rem(s + k, ns)
            copy_sub(send_s.at[phase, peer], recv_s.at[phase, s], phase, peer).start()
            return carry

        lax.fori_loop(1, ns, go, 0)
        down = copy_grp(send_f.at[phase, 0], recv_f.at[phase, 1], 4 + phase, prv)
        up = copy_grp(send_f.at[phase, 1], recv_f.at[phase, 0], 8 + phase, nxt)
        down.start()
        up.start()
        val_ref[0:PAIR, :] = got[PAIR : 2 * PAIR]
        val_ref[PAIR : 2 * PAIR, :] = got[0:PAIR]
        acc = scatter(0, 2, jnp.zeros((128, 128), F32))
        down.wait_recv()
        up.wait_recv()
        val_ref[at_face : at_face + FACE, :] = jnp.where(g == 0, 0.0, recv_f[phase, 0])
        val_ref[at_face + FACE :, :] = jnp.where(g == ng - 1, 0.0, recv_f[phase, 1])
        acc = scatter(tiles - 1, tiles, acc)
        wait_bytes(recv_s.at[phase, pl.ds(0, ns - 1)], recv_sem.at[phase])
        val_ref[2 * PAIR : at_face, :] = recv_s[phase].reshape(ns, 128)
        acc = scatter(2, tiles - 1, acc)
        return x + acc[:64] + acc[64:]

    def split(x):
        upper = x.astype(BF16)
        return upper, (x - upper.astype(F32)).astype(BF16)

    def dot(a, b):
        return jnp.dot(a, b, preferred_element_type=F32)

    def dot_right(x, k):
        upper, lower = split(x)
        both = dot(jnp.concatenate([upper, lower], axis=0), mats_ref[k])
        return both[:64] + both[64:] + dot(upper, mats_ref[k + 6])

    left_half = lax.broadcasted_iota(jnp.int32, (64, 128), 1) < 64

    def dot_rows(x, k):
        upper, lower = split(jnp.concatenate([x, pltpu.roll(x, 64, 1)], axis=0))
        both = dot(mats_ref[k], jnp.concatenate([upper, lower], axis=1))
        out = both[:, :128] + both[:, 128:] + dot(mats_ref[k + 6], upper)
        return jnp.where(left_half, out[:64], out[64:])

    def stiffness(x):
        flux_first = cube(metric_ref, 0) * dot_rows(x, 4)
        flux_second = cube(metric_ref, 512) * dot_right(x, 0)
        flux_third = cube(metric_ref, 1024) * dot_right(x, 1)
        return dot_rows(flux_first, 5) + dot_right(flux_second, 2) + dot_right(flux_third, 3)

    def operate(phase, x):
        summed = assemble(phase, x)
        return assemble(phase + 1, stiffness(summed)) + cube(helm_ref) * x

    direction = cube(jac_ref) * residual + prolong(coarse)
    rz_local = total(residual * direction)
    image = operate(0, direction)
    row = restrict(image) + put(64, rz_local) + put(65, total(direction * image))
    row = reduce_sub(1, row)
    sums = reduce_grp(0, row)
    rz_first, curved = pick(sums, 64), pick(sums, 65)
    alpha = rz_first / curved
    residual = residual - alpha * image
    coarse = coarse - alpha * row
    smoothed = cube(jac_ref) * residual + prolong(coarse)
    operated = operate(2, smoothed)
    row = (
        put(64, total(residual * smoothed))
        + put(65, total(smoothed * operated))
        + put(66, total(smoothed * image + direction * operated))
    )
    sums = reduce_grp(1, reduce_sub(2, row))
    rz_second = pick(sums, 64)
    beta = rz_second / rz_first
    curve = pick(sums, 65) + beta * pick(sums, 66) + beta * beta * curved
    alpha_last = rz_second / curve
    solved = alpha * direction + alpha_last * (smoothed + beta * direction)
    residual = residual - alpha_last * (operated + beta * image)
    for k in range(4):
        sol_ref[:, 128 * k : 128 * (k + 1)] = solved[16 * k : 16 * (k + 1)]
        res_ref[:, 128 * k : 128 * (k + 1)] = residual[16 * k : 16 * (k + 1)]

    for phase in range(4):
        wait_bytes(send_s.at[phase, pl.ds(0, ns - 1)], send_sem.at[phase])
        wait_bytes(send_f.at[phase, 0], send_sem.at[4 + phase])
        wait_bytes(send_f.at[phase, 1], send_sem.at[8 + phase])
    for phase in range(3):
        wait_bytes(recv_r.at[phase, pl.ds(0, ns - 1)], send_sem.at[12 + phase])
    for phase in range(2):
        wait_bytes(recv_b.at[phase, pl.ds(0, ng - 1)], send_sem.at[15 + phase])


def body(ns, ng, *args):
    mats, corner = tables()
    rows = 2 * PAIR + ns + 2 * FACE
    vmem = pl.BlockSpec(memory_space=pltpu.VMEM)
    shape = jax.ShapeDtypeStruct((16, 512), F32)
    return pl.pallas_call(
        functools.partial(kernel, ns, ng),
        out_shape=(shape, shape),
        in_specs=[vmem] * 11,
        out_specs=(vmem, vmem),
        scratch_shapes=[
            pltpu.VMEM((rows, 128), jnp.int32),
            pltpu.VMEM((rows, 128), jnp.int32),
            pltpu.VMEM((rows, 128), jnp.int32),
            pltpu.VMEM((rows // 8, 128, 1024), BF16),
            pltpu.VMEM((64, 128), F32),
            pltpu.VMEM((rows, 128), F32),
            pltpu.VMEM((64, 128), F32),
            pltpu.VMEM((8, 16, 128), F32),
            pltpu.VMEM((4, ns, 1, 128), F32),
            pltpu.VMEM((4, ns, 1, 128), F32),
            pltpu.VMEM((4, 2, FACE, 128), F32),
            pltpu.VMEM((4, 2, FACE, 128), F32),
            pltpu.VMEM((3, 1, 128), F32),
            pltpu.VMEM((3, ns, 1, 128), F32),
            pltpu.VMEM((2, 1, 128), F32),
            pltpu.VMEM((2, ng, 1, 128), F32),
            pltpu.SemaphoreType.DMA((17,)),
            pltpu.SemaphoreType.DMA((17,)),
        ],
        compiler_params=pltpu.CompilerParams(collective_id=0, has_side_effects=True),
    )(*args, mats, corner)


def solution(mesh):
    in_specs = (
        P(("grp", "sub"), None),
        P(("grp", "sub"), None),
        P(("grp", "sub"), None),
        P(("grp", "sub"), None),
        P(None, ("grp", "sub")),
        P(("grp", "sub"), None, None),
        P(None, ("grp", "sub")),
        P(None, ("grp", "sub")),
        P("grp", None, None),
    )
    out_specs = (P(("grp", "sub"), None), P(("grp", "sub"), None))
    return jax.shard_map(
        functools.partial(body, mesh.shape["sub"], mesh.shape["grp"]),
        mesh=mesh,
        in_specs=in_specs,
        out_specs=out_specs,
        check_vma=False,
    )
```

time: 945 us -> 83.8 us (0.09)
  blocking collectives: 426 us -> 0 us
  local copies, waits for them, and re-layouts: 242 us -> 2 us
  other arithmetic: 183 us -> 0 us
  Pallas kernels: 0 us -> 81 us
  starting transfers between devices: 63.1 us -> 0 us
    psum x5 -> x0, blocking collectives: 426 us -> none  [the longest x2 210 us: residual_product(): return lax.psum(jnp.sum(resid * smoothed), ('grp', 'sub'))]
    gather x16 -> x0, local copies, waits for them, and re-layouts: 236 us -> none  [the longest x4 162 us: assemble(): sent = padded[slots]]
    scatter-add x20 -> x0, other arithmetic: 181 us -> none  [the longest x4 105 us: assemble(): jnp.concatenate([total, jnp.zeros((1,), jnp.float32)]).at[slots]]
    pallas_call x0 -> x1, Pallas kernels: none -> 81 us  [body(): pl.pallas_call(functools.partial(kernel, ns, ng), out_shape=(shape, shape...]
    ppermute x8 -> x0, starting transfers between devices: 38.6 us -> none  [the longest x4 31 us: extended(): lax.ppermute(tail, axis, [(i, (i + 1) % count) for i in range(ends)])]
    all_to_all x4 -> x0, starting transfers between devices: 24.5 us -> none  [assemble(): lax.all_to_all(sent, 'sub', split_axis=0, concat_axis=0, tiled=True)]
  transfers between devices with their start and end apart: 12 -> 0, of which waited for: 3 -> 0; matrix products, arithmetic and copies ran while one was open for 16% -> 0% of each run, Pallas kernels for 0% -> 0%
where the time goes in v1:
time: 83.8 us; the launch traced here: 83.6 us
  Pallas kernels  81 us (97%)
  local copies, waits for them, and re-layouts  2 us (2%)
    pallas_call x1, Pallas kernels, body(): pl.pallas_call(functools.partial(kernel, ns, ng), out_shape=(shape, shape...  81 us
    unnamed x4, local copies, waits for them, and re-layouts  2 us

profile of v1, /device:TPU:1, one launch (start us, length us, event | category | flops | bytes accessed | tf_op | source)
XLA Modules:
  0.0 83.6 jit_solution(9409177350755490257)
XLA Ops:
  0.6 81.0 %shard_map.122 = (f32[16,512]{1,0:T(8,128)}, f32[16,512]{1,0:T(8,128)}) custom-call(f32[16,512]{1,0:T(8,128)} %right_ref.1, f32[16,1536]{1,0:T(8,128)} %metric_ref.1, f32[16,512]{1,0:T(8,128)} %helm_ref.1, f32[16,512]{1,0:T(8,128)} %jac_ref.1, s32[2,1024]{1,0:T(2,128)} %pair_ref.1, s32[1,32,128]{2,1,0:T(8,128)} %slots_ref.1, s32[2,512]{1,0:T(2,128)} %face_ref.1, ...), custom_call_target="tpu_custom_call" | custom-call | tf_op jit(solution)/shard_map/pallas_call | solution.py:409
  81.6 0.0 copy-start
  81.6 1.4 %copy.15 = f32[16,512]{1,0:T(8,128)} copy(f32[16,512]{1,0:T(8,128)} %get-tuple-element.4) | data formatting | bytes 65536
  83.0 0.0 copy-done
  83.0 0.6 copy.16
Async XLA Ops:
  81.6 1.4 %copy-start = (f32[16,512]{1,0:T(8,128)S(1)}, f32[16,512]{1,0:T(8,128)}, u32[]{:S(2)}) copy-start(f32[16,512]{1,0:T(8,128)} %get-tuple-element.5) | copy-start | bytes 98308

commit v2 on v1

--- a/solution.py
+++ b/solution.py
@@ -107,7 +107,7 @@
     nxt, prv = lax.rem(g + 1, ng), lax.rem(g + ng - 1, ng)
     rows = 2 * PAIR + ns + 2 * FACE
     tiles = rows // 8
-    at_face = 2 * PAIR + ns
+    at_pair = ns + 2 * FACE
 
     recv_s[...] = jnp.zeros_like(recv_s)
 
@@ -203,7 +203,7 @@
     def wait_bytes(ref, sem):
         pltpu.make_async_copy(ref, ref, sem).wait()
 
-    def reduce_sub(phase, row):
+    def sum_sub_start(phase, row):
         send_r[phase] = row
         recv_r[phase, s] = row
 
@@ -213,34 +213,37 @@
             return carry
 
         lax.fori_loop(1, ns, go, 0)
+
+    def sum_sub(phase):
         wait_bytes(recv_r.at[phase, pl.ds(0, ns - 1)], recv_sem.at[12 + phase])
         return jnp.sum(recv_r[phase], axis=0)
 
-    def reduce_grp(phase, row):
+    def sum_grp_start(phase, row):
         send_b[phase] = row
         recv_b[phase, g] = row
 
         def go(k, carry):
             peer = lax.rem(g + k, ng)
-            copy_grp(send_b.at[phase], recv_b.at[phase, g], 15 + phase, peer).start()
+            copy_grp(send_b.at[phase], recv_b.at[phase, g], 16 + phase, peer).start()
             return carry
 
         lax.fori_loop(1, ng, go, 0)
-        wait_bytes(recv_b.at[phase, pl.ds(0, ng - 1)], recv_sem.at[15 + phase])
+
+    def sum_grp(phase):
+        wait_bytes(recv_b.at[phase, pl.ds(0, ng - 1)], recv_sem.at[16 + phase])
         return jnp.sum(recv_b[phase], axis=0)
 
     residual = cube(right_ref)
     partial_coarse = restrict(residual)
 
-    for k in range(PAIR):
-        idx[k : k + 1, :] = pair_ref[0:1, 128 * k : 128 * (k + 1)]
-        idx[PAIR + k : PAIR + k + 1, :] = pair_ref[1:2, 128 * k : 128 * (k + 1)]
-    idx[2 * PAIR : at_face, :] = slots_ref[0]
-    for k in range(FACE):
-        idx[at_face + k : at_face + k + 1, :] = face_ref[0:1, 128 * k : 128 * (k + 1)]
-        idx[at_face + FACE + k : at_face + FACE + k + 1, :] = face_ref[
-            1:2, 128 * k : 128 * (k + 1)
-        ]
+    idx[:ns, :] = slots_ref[0]
+    for k in range(2):
+        for m in range(FACE):
+            at = ns + FACE * k + m
+            idx[at : at + 1, :] = face_ref[k : k + 1, 128 * m : 128 * (m + 1)]
+        for m in range(PAIR):
+            at = at_pair + PAIR * k + m
+            idx[at : at + 1, :] = pair_ref[k : k + 1, 128 * m : 128 * (m + 1)]
     points = idx[...]
     row_of = ((points >> 7) & 3) * 16 + (points >> 9)
     hi_ref[...] = jnp.where(points >= 8192, 1024, row_of)
@@ -248,7 +251,7 @@
 
     pl.semaphore_wait(barrier, ns + ng - 2)
 
-    coarse = reduce_sub(0, partial_coarse)
+    sum_sub_start(0, partial_coarse)
 
     sub_128 = lax.broadcasted_iota(jnp.int32, (128, 128), 0)
     sub_64 = lax.broadcasted_iota(jnp.int32, (64, 128), 0)
@@ -263,20 +266,19 @@
 
     lax.fori_loop(0, tiles, build, 0)
 
-    def gather(x):
-        x_ref[...] = x
-        high = hi_ref[...]
-        low = lo_ref[...]
+    def gather(first, last):
+        high = hi_ref[first:last, :]
+        low = lo_ref[first:last, :]
 
         def step(t, acc):
             block = x_ref[pl.ds(pl.multiple_of(t * 8, 8), 8), :]
             for r in range(8):
-                row = jnp.broadcast_to(block[r : r + 1], (rows, 128))
+                row = jnp.broadcast_to(block[r : r + 1], (last - first, 128))
                 got = jnp.take_along_axis(row, low, axis=1, mode="promise_in_bounds")
                 acc = jnp.where(high == t * 8 + r, got, acc)
             return acc
 
-        return lax.fori_loop(0, 8, step, jnp.zeros((rows, 128), F32))
+        return lax.fori_loop(0, 8, step, jnp.zeros((last - first, 128), F32))
 
     def scatter(first, last, acc):
         def step(t, acc):
@@ -304,11 +306,12 @@
 
         return lax.fori_loop(first, last, step, acc)
 
-    def assemble(phase, x):
-        got = gather(x)
-        send_s[phase] = got[2 * PAIR : at_face].reshape(ns, 1, 128)
-        send_f[phase, 0] = got[at_face : at_face + FACE]
-        send_f[phase, 1] = got[at_face + FACE :]
+    def assemble(phase, x, meanwhile=lambda: None, before_slots=lambda: None):
+        x_ref[...] = x
+        got = gather(0, at_pair)
+        send_s[phase] = got[:ns].reshape(ns, 1, 128)
+        send_f[phase, 0] = got[ns : ns + FACE]
+        send_f[phase, 1] = got[ns + FACE :]
 
         def go(k, carry):
             peer = lax.rem(s + k, ns)
@@ -320,17 +323,20 @@
         up = copy_grp(send_f.at[phase, 1], recv_f.at[phase, 0], 8 + phase, nxt)
         down.start()
         up.start()
-        val_ref[0:PAIR, :] = got[PAIR : 2 * PAIR]
-        val_ref[PAIR : 2 * PAIR, :] = got[0:PAIR]
-        acc = scatter(0, 2, jnp.zeros((128, 128), F32))
+        meanwhile()
+        got = gather(at_pair, rows)
+        val_ref[at_pair : at_pair + PAIR, :] = got[PAIR:]
+        val_ref[at_pair + PAIR :, :] = got[:PAIR]
+        acc = scatter(at_pair // 8, tiles, jnp.zeros((128, 128), F32))
         down.wait_recv()
         up.wait_recv()
-        val_ref[at_face : at_face + FACE, :] = jnp.where(g == 0, 0.0, recv_f[phase, 0])
-        val_ref[at_face + FACE :, :] = jnp.where(g == ng - 1, 0.0, recv_f[phase, 1])
-        acc = scatter(tiles - 1, tiles, acc)
+        val_ref[ns : ns + FACE, :] = jnp.where(g == 0, 0.0, recv_f[phase, 0])
+        val_ref[ns + FACE : at_pair, :] = jnp.where(g == ng - 1, 0.0, recv_f[phase, 1])
+        acc = scatter(ns // 8, at_pair // 8, acc)
+        before_slots()
         wait_bytes(recv_s.at[phase, pl.ds(0, ns - 1)], recv_sem.at[phase])
-        val_ref[2 * PAIR : at_face, :] = recv_s[phase].reshape(ns, 128)
-        acc = scatter(2, tiles - 1, acc)
+        val_ref[:ns, :] = recv_s[phase].reshape(ns, 128)
+        acc = scatter(0, ns // 8, acc)
         return x + acc[:64] + acc[64:]
 
     def split(x):
@@ -359,34 +365,53 @@
         flux_third = cube(metric_ref, 1024) * dot_right(x, 1)
         return dot_rows(flux_first, 5) + dot_right(flux_second, 2) + dot_right(flux_third, 3)
 
-    def operate(phase, x):
-        summed = assemble(phase, x)
-        return assemble(phase + 1, stiffness(summed)) + cube(helm_ref) * x
-
-    direction = cube(jac_ref) * residual + prolong(coarse)
-    rz_local = total(residual * direction)
-    image = operate(0, direction)
-    row = restrict(image) + put(64, rz_local) + put(65, total(direction * image))
-    row = reduce_sub(1, row)
-    sums = reduce_grp(0, row)
-    rz_first, curved = pick(sums, 64), pick(sums, 65)
+    right = residual
+    first = cube(jac_ref) * right + prolong(sum_sub(0))
+    summed = assemble(0, first)
+    inner = stiffness(summed)
+    mass = cube(helm_ref) * first
+
+    def first_sums():
+        row = put(0, total(right * first)) + put(1, total(summed * inner + first * mass))
+        sum_sub_start(1, row)
+
+    image = assemble(1, inner, first_sums)
+    image += mass
+    sum_sub_start(2, restrict(image))
+    sum_grp_start(0, sum_sub(1))
+    second = cube(jac_ref) * image + prolong(sum_sub(2))
+    summed_second = assemble(2, second)
+    inner_second = stiffness(summed_second)
+    sums = sum_grp(0)
+    rz_first, curved = pick(sums, 0), pick(sums, 1)
     alpha = rz_first / curved
-    residual = residual - alpha * image
-    coarse = coarse - alpha * row
-    smoothed = cube(jac_ref) * residual + prolong(coarse)
-    operated = operate(2, smoothed)
+    residual = right - alpha * image
+    smoothed = first - alpha * second
     row = (
-        put(64, total(residual * smoothed))
-        + put(65, total(smoothed * operated))
-        + put(66, total(smoothed * image + direction * operated))
-    )
-    sums = reduce_grp(1, reduce_sub(2, row))
-    rz_second = pick(sums, 64)
+        put(0, total(residual * smoothed))
+        + put(1, total(smoothed * image))
+        + put(
+            2,
+            total(
+                (summed - alpha * summed_second) * (inner - alpha * inner_second)
+                + smoothed * (cube(helm_ref) * smoothed)
+            ),
+        )
+    )
+    sum_sub_start(3, row)
+
+    def last_sums():
+        sum_grp_start(1, sum_sub(3))
+
+    image_second = assemble(3, inner_second, before_slots=last_sums)
+    image_second += cube(helm_ref) * second
+    sums = sum_grp(1)
+    rz_second = pick(sums, 0)
     beta = rz_second / rz_first
-    curve = pick(sums, 65) + beta * pick(sums, 66) + beta * beta * curved
+    curve = pick(sums, 2) + 2.0 * beta * pick(sums, 1) + beta * beta * curved
     alpha_last = rz_second / curve
-    solved = alpha * direction + alpha_last * (smoothed + beta * direction)
-    residual = residual - alpha_last * (operated + beta * image)
+    solved = alpha * first + alpha_last * (smoothed + beta * first)
+    residual = residual - alpha_last * (image - alpha * image_second + beta * image)
     for k in range(4):
         sol_ref[:, 128 * k : 128 * (k + 1)] = solved[16 * k : 16 * (k + 1)]
         res_ref[:, 128 * k : 128 * (k + 1)] = residual[16 * k : 16 * (k + 1)]
@@ -395,10 +420,10 @@
         wait_bytes(send_s.at[phase, pl.ds(0, ns - 1)], send_sem.at[phase])
         wait_bytes(send_f.at[phase, 0], send_sem.at[4 + phase])
         wait_bytes(send_f.at[phase, 1], send_sem.at[8 + phase])
-    for phase in range(3):
+    for phase in range(4):
         wait_bytes(recv_r.at[phase, pl.ds(0, ns - 1)], send_sem.at[12 + phase])
     for phase in range(2):
-        wait_bytes(recv_b.at[phase, pl.ds(0, ng - 1)], send_sem.at[15 + phase])
+        wait_bytes(recv_b.at[phase, pl.ds(0, ng - 1)], send_sem.at[16 + phase])
 
 
 def body(ns, ng, *args):
@@ -424,12 +449,12 @@
             pltpu.VMEM((4, ns, 1, 128), F32),
             pltpu.VMEM((4, 2, FACE, 128), F32),
             pltpu.VMEM((4, 2, FACE, 128), F32),
-            pltpu.VMEM((3, 1, 128), F32),
-            pltpu.VMEM((3, ns, 1, 128), F32),
+            pltpu.VMEM((4, 1, 128), F32),
+            pltpu.VMEM((4, ns, 1, 128), F32),
             pltpu.VMEM((2, 1, 128), F32),
             pltpu.VMEM((2, ng, 1, 128), F32),
-            pltpu.SemaphoreType.DMA((17,)),
-            pltpu.SemaphoreType.DMA((17,)),
+            pltpu.SemaphoreType.DMA((18,)),
+            pltpu.SemaphoreType.DMA((18,)),
         ],
         compiler_params=pltpu.CompilerParams(collective_id=0, has_side_effects=True),
     )(*args, mats, corner)

time: 83.8 us -> 70 us (0.84)
  Pallas kernels: 81 us -> 67.1 us
    pallas_call x1, Pallas kernels: 81 us -> 67.1 us  [body(): pl.pallas_call(functools.partial(kernel, ns, ng), out_shape=(shape, shape...]
where the time goes in v2:
time: 70 us; the launch traced here: 69.8 us
  Pallas kernels  67.1 us (96%)
  local copies, waits for them, and re-layouts  2 us (3%)
    pallas_call x1, Pallas kernels, body(): pl.pallas_call(functools.partial(kernel, ns, ng), out_shape=(shape, shape...  67.1 us
    unnamed x4, local copies, waits for them, and re-layouts  2 us

profile of v2, /device:TPU:1, one launch (start us, length us, event | category | flops | bytes accessed | tf_op | source)
XLA Modules:
  0.0 69.8 jit_solution(1320635172968807087)
XLA Ops:
  0.6 67.1 %shard_map.122 = (f32[16,512]{1,0:T(8,128)}, f32[16,512]{1,0:T(8,128)}) custom-call(f32[16,512]{1,0:T(8,128)} %right_ref.1, f32[16,1536]{1,0:T(8,128)} %metric_ref.1, f32[16,512]{1,0:T(8,128)} %helm_ref.1, f32[16,512]{1,0:T(8,128)} %jac_ref.1, s32[2,1024]{1,0:T(2,128)} %pair_ref.1, s32[1,32,128]{2,1,0:T(8,128)} %slots_ref.1, s32[2,512]{1,0:T(2,128)} %face_ref.1, ...), custom_call_target="tpu_custom_call" | custom-call | tf_op jit(solution)/shard_map/pallas_call | solution.py:434
  67.8 0.0 copy-start
  67.8 1.4 %copy.15 = f32[16,512]{1,0:T(8,128)} copy(f32[16,512]{1,0:T(8,128)} %get-tuple-element.4) | data formatting | bytes 65536
  69.2 0.0 copy-done
  69.2 0.6 copy.16
Async XLA Ops:
  67.8 1.4 %copy-start = (f32[16,512]{1,0:T(8,128)S(1)}, f32[16,512]{1,0:T(8,128)}, u32[]{:S(2)}) copy-start(f32[16,512]{1,0:T(8,128)} %get-tuple-element.5) | copy-start | bytes 98308

commit v3 on v2

--- a/solution.py
+++ b/solution.py
@@ -64,7 +64,10 @@
         * (0.5 * (1.0 + sign_second[None, :] * node_second))
         * (0.5 * (1.0 + sign_third[None, :] * node_third))
     )
-    return jnp.asarray(mats), jnp.asarray(corner.T, F32)
+    factors = np.zeros((8, 512))
+    factors[0, :8] = 0.5 * (1.0 + colloc)
+    factors[0, 8:16] = 0.5 * (1.0 - colloc)
+    return jnp.asarray(mats), jnp.asarray(np.concatenate([corner.T, factors]), F32)
 
 
 def kernel(
@@ -99,6 +102,12 @@
     recv_r,
     send_b,
     recv_b,
+    send_h,
+    recv_h,
+    send_t,
+    recv_t,
+    map_scr,
+    phi,
     send_sem,
     recv_sem,
 ):
@@ -110,6 +119,8 @@
     at_pair = ns + 2 * FACE
 
     recv_s[...] = jnp.zeros_like(recv_s)
+    recv_h[...] = jnp.zeros_like(recv_h)
+    recv_t[...] = jnp.zeros_like(recv_t)
 
     barrier = pltpu.get_barrier_semaphore()
 
@@ -170,9 +181,11 @@
         jnp.int32, (64, 128), 1
     )
 
-    def prolong(coarse):
+    def solve(coarse):
         column = jnp.sum(jnp.where(eye_64, coarse, 0.0), axis=1, keepdims=True)
-        solved = jnp.sum(cscr[...] * column, axis=0, keepdims=True)
+        return jnp.sum(cscr[...] * column, axis=0, keepdims=True)
+
+    def prolong(solved):
         blocks = [jnp.zeros((16, 128), F32) for _ in range(4)]
         for q in range(8):
             at_vertex = jnp.sum(mcol[q] * solved, axis=1, keepdims=True)
@@ -249,23 +262,6 @@
     hi_ref[...] = jnp.where(points >= 8192, 1024, row_of)
     lo_ref[...] = points & 127
 
-    pl.semaphore_wait(barrier, ns + ng - 2)
-
-    sum_sub_start(0, partial_coarse)
-
-    sub_128 = lax.broadcasted_iota(jnp.int32, (128, 128), 0)
-    sub_64 = lax.broadcasted_iota(jnp.int32, (64, 128), 0)
-
-    def build(t, carry):
-        low = lo_ref[pl.ds(pl.multiple_of(t * 8, 8), 8), :]
-        ohlo[t] = jnp.concatenate(
-            [jnp.where(sub_128 == low[r : r + 1], 1.0, 0.0).astype(BF16) for r in range(8)],
-            axis=1,
-        )
-        return carry
-
-    lax.fori_loop(0, tiles, build, 0)
-
     def gather(first, last):
         high = hi_ref[first:last, :]
         low = lo_ref[first:last, :]
@@ -279,6 +275,47 @@
             return acc
 
         return lax.fori_loop(0, 8, step, jnp.zeros((last - first, 128), F32))
+
+    def look(table, at):
+        return jnp.take_along_axis(table, at, axis=1, mode="promise_in_bounds")
+
+    map_scr[...] = jnp.zeros_like(map_scr)
+    map_scr[:, :16] = map_ref[...]
+    lane_8 = lax.broadcasted_iota(jnp.int32, (8, 128), 1)
+    corner_row = lax.broadcasted_iota(jnp.int32, (8, 128), 0) == lane_8 >> 4
+    spread = look(map_scr[...], lane_8 & 15).astype(F32)
+    map_row = jnp.sum(jnp.where(corner_row, spread, 0.0), axis=0, keepdims=True)
+    x_ref[...] = cube(jac_ref) * residual
+    send_h[:, :, :128] = jnp.broadcast_to(partial_coarse.reshape(1, 1, 128), (ns, 1, 128))
+    send_h[:, :, 128:] = gather(0, ns).reshape(ns, 1, 128)
+    send_t[:, :, :128] = jnp.broadcast_to(
+        map_row.astype(jnp.int32).reshape(1, 1, 128), (ns, 1, 128)
+    )
+    send_t[:, :, 128:] = points[:ns].reshape(ns, 1, 128)
+    recv_h[s, :, :128] = partial_coarse
+
+    pl.semaphore_wait(barrier, ns + ng - 2)
+
+    def hello(k, carry):
+        peer = lax.rem(s + k, ns)
+        copy_sub(send_h.at[peer], recv_h.at[s], 18, peer).start()
+        copy_sub(send_t.at[peer], recv_t.at[s], 19, peer).start()
+        return carry
+
+    lax.fori_loop(1, ns, hello, 0)
+
+    sub_128 = lax.broadcasted_iota(jnp.int32, (128, 128), 0)
+    sub_64 = lax.broadcasted_iota(jnp.int32, (64, 128), 0)
+
+    def build(t, carry):
+        low = lo_ref[pl.ds(pl.multiple_of(t * 8, 8), 8), :]
+        ohlo[t] = jnp.concatenate(
+            [jnp.where(sub_128 == low[r : r + 1], 1.0, 0.0).astype(BF16) for r in range(8)],
+            axis=1,
+        )
+        return carry
+
+    lax.fori_loop(0, tiles, build, 0)
 
     def scatter(first, last, acc):
         def step(t, acc):
@@ -306,12 +343,8 @@
 
         return lax.fori_loop(first, last, step, acc)
 
-    def assemble(phase, x, meanwhile=lambda: None, before_slots=lambda: None):
-        x_ref[...] = x
-        got = gather(0, at_pair)
-        send_s[phase] = got[:ns].reshape(ns, 1, 128)
-        send_f[phase, 0] = got[ns : ns + FACE]
-        send_f[phase, 1] = got[ns + FACE :]
+    def send_slots(phase):
+        send_s[phase] = gather(0, ns).reshape(ns, 1, 128)
 
         def go(k, carry):
             peer = lax.rem(s + k, ns)
@@ -319,25 +352,73 @@
             return carry
 
         lax.fori_loop(1, ns, go, 0)
+
+    def send_faces(phase):
+        got = gather(ns, at_pair)
+        send_f[phase, 0] = got[:FACE]
+        send_f[phase, 1] = got[FACE:]
         down = copy_grp(send_f.at[phase, 0], recv_f.at[phase, 1], 4 + phase, prv)
         up = copy_grp(send_f.at[phase, 1], recv_f.at[phase, 0], 8 + phase, nxt)
         down.start()
         up.start()
-        meanwhile()
+        return down, up
+
+    def add_pairs():
         got = gather(at_pair, rows)
         val_ref[at_pair : at_pair + PAIR, :] = got[PAIR:]
         val_ref[at_pair + PAIR :, :] = got[:PAIR]
-        acc = scatter(at_pair // 8, tiles, jnp.zeros((128, 128), F32))
-        down.wait_recv()
-        up.wait_recv()
+        return scatter(at_pair // 8, tiles, jnp.zeros((128, 128), F32))
+
+    def add_faces(phase, copies, acc):
+        for copy in copies:
+            copy.wait_recv()
         val_ref[ns : ns + FACE, :] = jnp.where(g == 0, 0.0, recv_f[phase, 0])
         val_ref[ns + FACE : at_pair, :] = jnp.where(g == ng - 1, 0.0, recv_f[phase, 1])
-        acc = scatter(ns // 8, at_pair // 8, acc)
+        return scatter(ns // 8, at_pair // 8, acc)
+
+    def wait_slots(phase):
+        wait_bytes(recv_s.at[phase, pl.ds(0, ns - 1)], recv_sem.at[phase])
+        return recv_s[phase].reshape(ns, 128)
+
+    def add_slots(value, acc):
+        val_ref[:ns, :] = value
+        return scatter(0, ns // 8, acc)
+
+    def assemble(phase, x, meanwhile=lambda: None, before_slots=lambda: None):
+        x_ref[...] = x
+        send_slots(phase)
+        copies = send_faces(phase)
+        meanwhile()
+        acc = add_faces(phase, copies, add_pairs())
         before_slots()
-        wait_bytes(recv_s.at[phase, pl.ds(0, ns - 1)], recv_sem.at[phase])
-        val_ref[:ns, :] = recv_s[phase].reshape(ns, 128)
-        acc = scatter(0, ns // 8, acc)
+        acc = add_slots(wait_slots(phase), acc)
         return x + acc[:64] + acc[64:]
+
+    def assemble_known(phase, x, slot_values):
+        x_ref[...] = x
+        copies = send_faces(phase)
+        acc = add_slots(slot_values, add_pairs())
+        acc = add_faces(phase, copies, acc)
+        return x + acc[:64] + acc[64:]
+
+    def peer_points():
+        return recv_t[:, :, 128:].reshape(ns, 128)
+
+    def corner_functions():
+        point = peer_points()
+        table = jnp.broadcast_to(corner_ref[8:9, :128], (ns, 128))
+        nodes = [(point >> 6) & 7, (point >> 3) & 7, point & 7]
+        near = [[look(table, node + 8 * bit) for bit in range(2)] for node in nodes]
+        for q in range(8):
+            phi[q] = near[0][q >> 2 & 1] * near[1][q >> 1 & 1] * near[2][q & 1]
+
+    def coarse_at_peers(solved):
+        corners = look(jnp.broadcast_to(solved, (ns, 128)), recv_t[:, :, :128].reshape(ns, 128))
+        element = (peer_points() >> 9) & 15
+        out = jnp.zeros((ns, 128), F32)
+        for q in range(8):
+            out += phi[q] * look(corners, element + 16 * q)
+        return out
 
     def split(x):
         upper = x.astype(BF16)
@@ -366,8 +447,15 @@
         return dot_rows(flux_first, 5) + dot_right(flux_second, 2) + dot_right(flux_third, 3)
 
     right = residual
-    first = cube(jac_ref) * right + prolong(sum_sub(0))
-    summed = assemble(0, first)
+    part = cube(jac_ref) * right
+    wait_bytes(recv_t.at[pl.ds(0, ns - 1)], recv_sem.at[19])
+    corner_functions()
+    wait_bytes(recv_h.at[pl.ds(0, ns - 1)], recv_sem.at[18])
+    solved = solve(jnp.sum(recv_h[:, :, :128], axis=0))
+    first = part + prolong(solved)
+    summed = assemble_known(
+        0, first, recv_h[:, :, 128:].reshape(ns, 128) + coarse_at_peers(solved)
+    )
     inner = stiffness(summed)
     mass = cube(helm_ref) * first
 
@@ -378,9 +466,14 @@
     image = assemble(1, inner, first_sums)
     image += mass
     sum_sub_start(2, restrict(image))
+    part = cube(jac_ref) * image
+    x_ref[...] = part
+    send_slots(2)
     sum_grp_start(0, sum_sub(1))
-    second = cube(jac_ref) * image + prolong(sum_sub(2))
-    summed_second = assemble(2, second)
+    solved = solve(sum_sub(2))
+    second = part + prolong(solved)
+    known = coarse_at_peers(solved)
+    summed_second = assemble_known(2, second, wait_slots(2) + known)
     inner_second = stiffness(summed_second)
     sums = sum_grp(0)
     rz_first, curved = pick(sums, 0), pick(sums, 1)
@@ -416,11 +509,14 @@
         sol_ref[:, 128 * k : 128 * (k + 1)] = solved[16 * k : 16 * (k + 1)]
         res_ref[:, 128 * k : 128 * (k + 1)] = residual[16 * k : 16 * (k + 1)]
 
+    for phase in range(1, 4):
+        wait_bytes(send_s.at[phase, pl.ds(0, ns - 1)], send_sem.at[phase])
     for phase in range(4):
-        wait_bytes(send_s.at[phase, pl.ds(0, ns - 1)], send_sem.at[phase])
         wait_bytes(send_f.at[phase, 0], send_sem.at[4 + phase])
         wait_bytes(send_f.at[phase, 1], send_sem.at[8 + phase])
-    for phase in range(4):
+    wait_bytes(send_h.at[pl.ds(0, ns - 1)], send_sem.at[18])
+    wait_bytes(send_t.at[pl.ds(0, ns - 1)], send_sem.at[19])
+    for phase in range(1, 4):
         wait_bytes(recv_r.at[phase, pl.ds(0, ns - 1)], send_sem.at[12 + phase])
     for phase in range(2):
         wait_bytes(recv_b.at[phase, pl.ds(0, ng - 1)], send_sem.at[16 + phase])
@@ -453,8 +549,14 @@
             pltpu.VMEM((4, ns, 1, 128), F32),
             pltpu.VMEM((2, 1, 128), F32),
             pltpu.VMEM((2, ng, 1, 128), F32),
-            pltpu.SemaphoreType.DMA((18,)),
-            pltpu.SemaphoreType.DMA((18,)),
+            pltpu.VMEM((ns, 1, 256), F32),
+            pltpu.VMEM((ns, 1, 256), F32),
+            pltpu.VMEM((ns, 1, 256), jnp.int32),
+            pltpu.VMEM((ns, 1, 256), jnp.int32),
+            pltpu.VMEM((8, 128), jnp.int32),
+            pltpu.VMEM((8, ns, 128), F32),
+            pltpu.SemaphoreType.DMA((20,)),
+            pltpu.SemaphoreType.DMA((20,)),
         ],
         compiler_params=pltpu.CompilerParams(collective_id=0, has_side_effects=True),
     )(*args, mats, corner)

time: 70 us -> 62.2 us (0.89)
  Pallas kernels: 67.1 us -> 59.3 us
    pallas_call x1, Pallas kernels: 67.1 us -> 59.3 us  [body(): pl.pallas_call(functools.partial(kernel, ns, ng), out_shape=(shape, shape...]
where the time goes in v3:
time: 62.2 us; the launch traced here: 61.9 us
  Pallas kernels  59.3 us (95%)
  local copies, waits for them, and re-layouts  2 us (3%)
  between operations  0.65 us (1%)
    pallas_call x1, Pallas kernels, body(): pl.pallas_call(functools.partial(kernel, ns, ng), out_shape=(shape, shape...  59.3 us
    unnamed x4, local copies, waits for them, and re-layouts  2 us

profile of v3, /device:TPU:1, one launch (start us, length us, event | category | flops | bytes accessed | tf_op | source)
XLA Modules:
  0.0 61.9 jit_solution(3421336072471551522)
XLA Ops:
  0.6 59.3 %shard_map.122 = (f32[16,512]{1,0:T(8,128)}, f32[16,512]{1,0:T(8,128)}) custom-call(f32[16,512]{1,0:T(8,128)} %right_ref.1, f32[16,1536]{1,0:T(8,128)} %metric_ref.1, f32[16,512]{1,0:T(8,128)} %helm_ref.1, f32[16,512]{1,0:T(8,128)} %jac_ref.1, s32[2,1024]{1,0:T(2,128)} %pair_ref.1, s32[1,32,128]{2,1,0:T(8,128)} %slots_ref.1, s32[2,512]{1,0:T(2,128)} %face_ref.1, ...), custom_call_target="tpu_custom_call" | custom-call | tf_op jit(solution)/shard_map/pallas_call | solution.py:530
  59.9 0.0 copy-start
  60.0 1.4 %copy.15 = f32[16,512]{1,0:T(8,128)} copy(f32[16,512]{1,0:T(8,128)} %get-tuple-element.4) | data formatting | bytes 65536
  61.3 0.0 copy-done
  61.3 0.6 copy.16
Async XLA Ops:
  59.9 1.4 %copy-start = (f32[16,512]{1,0:T(8,128)S(1)}, f32[16,512]{1,0:T(8,128)}, u32[]{:S(2)}) copy-start(f32[16,512]{1,0:T(8,128)} %get-tuple-element.5) | copy-start | bytes 98308

commit v4 on v3

--- a/solution.py
+++ b/solution.py
@@ -136,8 +136,8 @@
         )
         return carry
 
-    lax.fori_loop(1, ns, greet_sub, 0)
-    lax.fori_loop(1, ng, greet_grp, 0)
+    lax.fori_loop(1, ns, greet_sub, 0, unroll=True)
+    lax.fori_loop(1, ng, greet_grp, 0, unroll=True)
 
     def cube(ref, base=0):
         return jnp.concatenate(
@@ -225,7 +225,7 @@
             copy_sub(send_r.at[phase], recv_r.at[phase, s], 12 + phase, peer).start()
             return carry
 
-        lax.fori_loop(1, ns, go, 0)
+        lax.fori_loop(1, ns, go, 0, unroll=True)
 
     def sum_sub(phase):
         wait_bytes(recv_r.at[phase, pl.ds(0, ns - 1)], recv_sem.at[12 + phase])
@@ -240,7 +240,7 @@
             copy_grp(send_b.at[phase], recv_b.at[phase, g], 16 + phase, peer).start()
             return carry
 
-        lax.fori_loop(1, ng, go, 0)
+        lax.fori_loop(1, ng, go, 0, unroll=True)
 
     def sum_grp(phase):
         wait_bytes(recv_b.at[phase, pl.ds(0, ng - 1)], recv_sem.at[16 + phase])
@@ -274,7 +274,9 @@
                 acc = jnp.where(high == t * 8 + r, got, acc)
             return acc
 
-        return lax.fori_loop(0, 8, step, jnp.zeros((last - first, 128), F32))
+        return lax.fori_loop(
+            0, 8, step, jnp.zeros((last - first, 128), F32), unroll=True
+        )
 
     def look(table, at):
         return jnp.take_along_axis(table, at, axis=1, mode="promise_in_bounds")
@@ -302,7 +304,7 @@
         copy_sub(send_t.at[peer], recv_t.at[s], 19, peer).start()
         return carry
 
-    lax.fori_loop(1, ns, hello, 0)
+    lax.fori_loop(1, ns, hello, 0, unroll=True)
 
     sub_128 = lax.broadcasted_iota(jnp.int32, (128, 128), 0)
     sub_64 = lax.broadcasted_iota(jnp.int32, (64, 128), 0)
@@ -315,7 +317,7 @@
         )
         return carry
 
-    lax.fori_loop(0, tiles, build, 0)
+    lax.fori_loop(0, tiles, build, 0, unroll=True)
 
     def scatter(first, last, acc):
         def step(t, acc):
@@ -341,7 +343,7 @@
                 left, ohlo[t], (((1,), (1,)), ((), ())), preferred_element_type=F32
             )
 
-        return lax.fori_loop(first, last, step, acc)
+        return lax.fori_loop(first, last, step, acc, unroll=True)
 
     def send_slots(phase):
         send_s[phase] = gather(0, ns).reshape(ns, 1, 128)
@@ -351,7 +353,7 @@
             copy_sub(send_s.at[phase, peer], recv_s.at[phase, s], phase, peer).start()
             return carry
 
-        lax.fori_loop(1, ns, go, 0)
+        lax.fori_loop(1, ns, go, 0, unroll=True)
 
     def send_faces(phase):
         got = gather(ns, at_pair)

time: 62.2 us -> 58.9 us (0.947)
  Pallas kernels: 59.3 us -> 56 us
    pallas_call x1, Pallas kernels: 59.3 us -> 56 us  [body(): pl.pallas_call(functools.partial(kernel, ns, ng), out_shape=(shape, shape...]
where the time goes in v4:
time: 58.9 us; the launch traced here: 58.7 us
  Pallas kernels  56 us (95%)
  local copies, waits for them, and re-layouts  2 us (3%)
  between operations  0.65 us (1%)
    pallas_call x1, Pallas kernels, body(): pl.pallas_call(functools.partial(kernel, ns, ng), out_shape=(shape, shape...  56 us
    unnamed x4, local copies, waits for them, and re-layouts  2 us

profile of v4, /device:TPU:1, one launch (start us, length us, event | category | flops | bytes accessed | tf_op | source)
XLA Modules:
  0.0 58.7 jit_solution(13397363247408765136)
XLA Ops:
  0.6 56.0 %shard_map.122 = (f32[16,512]{1,0:T(8,128)}, f32[16,512]{1,0:T(8,128)}) custom-call(f32[16,512]{1,0:T(8,128)} %right_ref.1, f32[16,1536]{1,0:T(8,128)} %metric_ref.1, f32[16,512]{1,0:T(8,128)} %helm_ref.1, f32[16,512]{1,0:T(8,128)} %jac_ref.1, s32[2,1024]{1,0:T(2,128)} %pair_ref.1, s32[1,32,128]{2,1,0:T(8,128)} %slots_ref.1, s32[2,512]{1,0:T(2,128)} %face_ref.1, ...), custom_call_target="tpu_custom_call" | custom-call | tf_op jit(solution)/shard_map/pallas_call | solution.py:532
  56.7 0.0 copy-start
  56.7 1.4 %copy.15 = f32[16,512]{1,0:T(8,128)} copy(f32[16,512]{1,0:T(8,128)} %get-tuple-element.4) | data formatting | bytes 65536
  58.1 0.0 copy-done
  58.1 0.6 %copy.16 = f32[16,512]{1,0:T(8,128)} copy(f32[16,512]{1,0:T(8,128)S(1)} %copy-done) | data formatting | bytes 65536
Async XLA Ops:
  56.7 1.4 %copy-start = (f32[16,512]{1,0:T(8,128)S(1)}, f32[16,512]{1,0:T(8,128)}, u32[]{:S(2)}) copy-start(f32[16,512]{1,0:T(8,128)} %get-tuple-element.5) | copy-start | bytes 98308

commit v5 on v4

--- a/solution.py
+++ b/solution.py
@@ -84,8 +84,7 @@
     cinv_ref,
     mats_ref,
     corner_ref,
-    sol_ref,
-    res_ref,
+    out_ref,
     idx,
     hi_ref,
     lo_ref,
@@ -301,10 +300,15 @@
     def hello(k, carry):
         peer = lax.rem(s + k, ns)
         copy_sub(send_h.at[peer], recv_h.at[s], 18, peer).start()
+        return carry
+
+    def hello_tables(k, carry):
+        peer = lax.rem(s + k, ns)
         copy_sub(send_t.at[peer], recv_t.at[s], 19, peer).start()
         return carry
 
     lax.fori_loop(1, ns, hello, 0, unroll=True)
+    lax.fori_loop(1, ns, hello_tables, 0, unroll=True)
 
     sub_128 = lax.broadcasted_iota(jnp.int32, (128, 128), 0)
     sub_64 = lax.broadcasted_iota(jnp.int32, (64, 128), 0)
@@ -399,7 +403,8 @@
     def assemble_known(phase, x, slot_values):
         x_ref[...] = x
         copies = send_faces(phase)
-        acc = add_slots(slot_values, add_pairs())
+        acc = add_pairs()
+        acc = add_slots(slot_values(), acc)
         acc = add_faces(phase, copies, acc)
         return x + acc[:64] + acc[64:]
 
@@ -450,14 +455,16 @@
 
     right = residual
     part = cube(jac_ref) * right
-    wait_bytes(recv_t.at[pl.ds(0, ns - 1)], recv_sem.at[19])
-    corner_functions()
     wait_bytes(recv_h.at[pl.ds(0, ns - 1)], recv_sem.at[18])
     solved = solve(jnp.sum(recv_h[:, :, :128], axis=0))
     first = part + prolong(solved)
-    summed = assemble_known(
-        0, first, recv_h[:, :, 128:].reshape(ns, 128) + coarse_at_peers(solved)
-    )
+
+    def first_slots():
+        wait_bytes(recv_t.at[pl.ds(0, ns - 1)], recv_sem.at[19])
+        corner_functions()
+        return recv_h[:, :, 128:].reshape(ns, 128) + coarse_at_peers(solved)
+
+    summed = assemble_known(0, first, first_slots)
     inner = stiffness(summed)
     mass = cube(helm_ref) * first
 
@@ -472,10 +479,14 @@
     x_ref[...] = part
     send_slots(2)
     sum_grp_start(0, sum_sub(1))
-    solved = solve(sum_sub(2))
-    second = part + prolong(solved)
-    known = coarse_at_peers(solved)
-    summed_second = assemble_known(2, second, wait_slots(2) + known)
+    solved_second = solve(sum_sub(2))
+    second = part + prolong(solved_second)
+
+    def second_slots():
+        known = coarse_at_peers(solved_second)
+        return wait_slots(2) + known
+
+    summed_second = assemble_known(2, second, second_slots)
     inner_second = stiffness(summed_second)
     sums = sum_grp(0)
     rz_first, curved = pick(sums, 0), pick(sums, 1)
@@ -508,8 +519,8 @@
     solved = alpha * first + alpha_last * (smoothed + beta * first)
     residual = residual - alpha_last * (image - alpha * image_second + beta * image)
     for k in range(4):
-        sol_ref[:, 128 * k : 128 * (k + 1)] = solved[16 * k : 16 * (k + 1)]
-        res_ref[:, 128 * k : 128 * (k + 1)] = residual[16 * k : 16 * (k + 1)]
+        out_ref[0, :, 128 * k : 128 * (k + 1)] = solved[16 * k : 16 * (k + 1)]
+        out_ref[1, :, 128 * k : 128 * (k + 1)] = residual[16 * k : 16 * (k + 1)]
 
     for phase in range(1, 4):
         wait_bytes(send_s.at[phase, pl.ds(0, ns - 1)], send_sem.at[phase])
@@ -529,11 +540,11 @@
     rows = 2 * PAIR + ns + 2 * FACE
     vmem = pl.BlockSpec(memory_space=pltpu.VMEM)
     shape = jax.ShapeDtypeStruct((16, 512), F32)
-    return pl.pallas_call(
+    out = pl.pallas_call(
         functools.partial(kernel, ns, ng),
-        out_shape=(shape, shape),
+        out_shape=jax.ShapeDtypeStruct((2, 16, 512), F32),
         in_specs=[vmem] * 11,
-        out_specs=(vmem, vmem),
+        out_specs=vmem,
         scratch_shapes=[
             pltpu.VMEM((rows, 128), jnp.int32),
             pltpu.VMEM((rows, 128), jnp.int32),
@@ -562,6 +573,7 @@
         ],
         compiler_params=pltpu.CompilerParams(collective_id=0, has_side_effects=True),
     )(*args, mats, corner)
+    return out[0], out[1]
 
 
 def solution(mesh):

time: 58.9 us -> 56.7 us (0.963)
  Pallas kernels: 56 us -> 54.4 us
  local copies, waits for them, and re-layouts: 2 us -> 1.41 us
    unnamed x4 -> x0, local copies, waits for them, and re-layouts: 2 us -> none
    pallas_call x1, Pallas kernels: 56 us -> 54.4 us  [body(): pl.pallas_call(functools.partial(kernel, ns, ng), out_shape=jax.ShapeDtyp...]
    squeeze x0 -> x1, local copies, waits for them, and re-layouts: none -> 1.41 us  [body(): return (out[0], out[1])]
where the time goes in v5:
time: 56.7 us; the launch traced here: 56.5 us
  Pallas kernels  54.4 us (96%)
  local copies, waits for them, and re-layouts  1.41 us (2%)
  between operations  0.64 us (1%)
    pallas_call x1, Pallas kernels, body(): pl.pallas_call(functools.partial(kernel, ns, ng), out_shape=jax.ShapeDtyp...  54.4 us
    squeeze x1, local copies, waits for them, and re-layouts, body(): return (out[0], out[1])  1.41 us

profile of v5, /device:TPU:1, one launch (start us, length us, event | category | flops | bytes accessed | tf_op | source)
XLA Modules:
  0.0 56.5 jit_solution(10174404827029341543)
XLA Ops:
  0.6 54.4 %shard_map.122 = f32[2,16,512]{2,1,0:T(8,128)} custom-call(f32[16,512]{1,0:T(8,128)} %right_ref.1, f32[16,1536]{1,0:T(8,128)} %metric_ref.1, f32[16,512]{1,0:T(8,128)} %helm_ref.1, f32[16,512]{1,0:T(8,128)} %jac_ref.1, s32[2,1024]{1,0:T(2,128)} %pair_ref.1, s32[1,32,128]{2,1,0:T(8,128)} %slots_ref.1, s32[2,512]{1,0:T(2,128)} %face_ref.1, s32[8,16]{1,0:T(8,128)} %map_ref.1, ...), custom_call_target="tpu_custom_call" | custom-call | tf_op jit(solution)/shard_map/pallas_call | solution.py:543
  55.0 1.4 %slice_bitcast_fusion = (f32[16,512]{1,0:T(8,128)}, f32[16,512]{1,0:T(8,128)}) fusion(f32[2,16,512]{2,1,0:T(8,128)} %shard_map.122), kind=kLoop, calls=%fused_computation | loop fusion | bytes 131072 | tf_op jit(solution)/shard_map/squeeze | solution.py:576

commit v6 on v5

--- a/solution.py
+++ b/solution.py
@@ -121,22 +121,33 @@
     recv_h[...] = jnp.zeros_like(recv_h)
     recv_t[...] = jnp.zeros_like(recv_t)
 
+    def far_first(step, count):
+        return count // 2 + (1 - 2 * lax.rem(step, 2)) * lax.div(step + 1, 2)
+
+    def sub_peer(step):
+        row = lax.div(s, 4) + far_first(lax.div(step, 4), ns // 4)
+        column = lax.rem(s, 4) + far_first(lax.rem(step, 4), 4)
+        return lax.rem(row, ns // 4) * 4 + lax.rem(column, 4)
+
+    def grp_peer(step):
+        return lax.rem(g + far_first(step, ng), ng)
+
     barrier = pltpu.get_barrier_semaphore()
 
     def greet_sub(k, carry):
         pl.semaphore_signal(
-            barrier, inc=1, device_id={"sub": lax.rem(s + k, ns)}, device_id_type=MESH
+            barrier, inc=1, device_id={"sub": sub_peer(k)}, device_id_type=MESH
         )
         return carry
 
     def greet_grp(k, carry):
         pl.semaphore_signal(
-            barrier, inc=1, device_id={"grp": lax.rem(g + k, ng)}, device_id_type=MESH
+            barrier, inc=1, device_id={"grp": grp_peer(k)}, device_id_type=MESH
         )
         return carry
 
-    lax.fori_loop(1, ns, greet_sub, 0, unroll=True)
-    lax.fori_loop(1, ng, greet_grp, 0, unroll=True)
+    lax.fori_loop(0, ns - 1, greet_sub, 0, unroll=True)
+    lax.fori_loop(0, ng - 1, greet_grp, 0, unroll=True)
 
     def cube(ref, base=0):
         return jnp.concatenate(
@@ -220,11 +231,11 @@
         recv_r[phase, s] = row
 
         def go(k, carry):
-            peer = lax.rem(s + k, ns)
+            peer = sub_peer(k)
             copy_sub(send_r.at[phase], recv_r.at[phase, s], 12 + phase, peer).start()
             return carry
 
-        lax.fori_loop(1, ns, go, 0, unroll=True)
+        lax.fori_loop(0, ns - 1, go, 0, unroll=True)
 
     def sum_sub(phase):
         wait_bytes(recv_r.at[phase, pl.ds(0, ns - 1)], recv_sem.at[12 + phase])
@@ -235,11 +246,11 @@
         recv_b[phase, g] = row
 
         def go(k, carry):
-            peer = lax.rem(g + k, ng)
+            peer = grp_peer(k)
             copy_grp(send_b.at[phase], recv_b.at[phase, g], 16 + phase, peer).start()
             return carry
 
-        lax.fori_loop(1, ng, go, 0, unroll=True)
+        lax.fori_loop(0, ng - 1, go, 0, unroll=True)
 
     def sum_grp(phase):
         wait_bytes(recv_b.at[phase, pl.ds(0, ng - 1)], recv_sem.at[16 + phase])
@@ -298,17 +309,17 @@
     pl.semaphore_wait(barrier, ns + ng - 2)
 
     def hello(k, carry):
-        peer = lax.rem(s + k, ns)
+        peer = sub_peer(k)
         copy_sub(send_h.at[peer], recv_h.at[s], 18, peer).start()
         return carry
 
     def hello_tables(k, carry):
-        peer = lax.rem(s + k, ns)
+        peer = sub_peer(k)
         copy_sub(send_t.at[peer], recv_t.at[s], 19, peer).start()
         return carry
 
-    lax.fori_loop(1, ns, hello, 0, unroll=True)
-    lax.fori_loop(1, ns, hello_tables, 0, unroll=True)
+    lax.fori_loop(0, ns - 1, hello, 0, unroll=True)
+    lax.fori_loop(0, ns - 1, hello_tables, 0, unroll=True)
 
     sub_128 = lax.broadcasted_iota(jnp.int32, (128, 128), 0)
     sub_64 = lax.broadcasted_iota(jnp.int32, (64, 128), 0)
@@ -353,11 +364,11 @@
         send_s[phase] = gather(0, ns).reshape(ns, 1, 128)
 
         def go(k, carry):
-            peer = lax.rem(s + k, ns)
+            peer = sub_peer(k)
             copy_sub(send_s.at[phase, peer], recv_s.at[phase, s], phase, peer).start()
             return carry
 
-        lax.fori_loop(1, ns, go, 0, unroll=True)
+        lax.fori_loop(0, ns - 1, go, 0, unroll=True)
 
     def send_faces(phase):
         got = gather(ns, at_pair)

time: 56.7 us -> 55.8 us (0.984)
  Pallas kernels: 54.4 us -> 53.6 us
    pallas_call x1, Pallas kernels: 54.4 us -> 53.6 us  [body(): pl.pallas_call(functools.partial(kernel, ns, ng), out_shape=jax.ShapeDtyp...]
where the time goes in v6:
time: 55.8 us; the launch traced here: 55.6 us
  Pallas kernels  53.6 us (96%)
  local copies, waits for them, and re-layouts  1.41 us (3%)
  between operations  0.64 us (1%)
    pallas_call x1, Pallas kernels, body(): pl.pallas_call(functools.partial(kernel, ns, ng), out_shape=jax.ShapeDtyp...  53.6 us
    squeeze x1, local copies, waits for them, and re-layouts, body(): return (out[0], out[1])  1.41 us

profile of v6, /device:TPU:1, one launch (start us, length us, event | category | flops | bytes accessed | tf_op | source)
XLA Modules:
  0.0 55.6 jit_solution(18194424826906043143)
XLA Ops:
  0.6 53.6 %shard_map.122 = f32[2,16,512]{2,1,0:T(8,128)} custom-call(f32[16,512]{1,0:T(8,128)} %right_ref.1, f32[16,1536]{1,0:T(8,128)} %metric_ref.1, f32[16,512]{1,0:T(8,128)} %helm_ref.1, f32[16,512]{1,0:T(8,128)} %jac_ref.1, s32[2,1024]{1,0:T(2,128)} %pair_ref.1, s32[1,32,128]{2,1,0:T(8,128)} %slots_ref.1, s32[2,512]{1,0:T(2,128)} %face_ref.1, s32[8,16]{1,0:T(8,128)} %map_ref.1, ...), custom_call_target="tpu_custom_call" | custom-call | tf_op jit(solution)/shard_map/pallas_call | solution.py:554
  54.2 1.4 %slice_bitcast_fusion = (f32[16,512]{1,0:T(8,128)}, f32[16,512]{1,0:T(8,128)}) fusion(f32[2,16,512]{2,1,0:T(8,128)} %shard_map.122), kind=kLoop, calls=%fused_computation | loop fusion | bytes 131072 | tf_op jit(solution)/shard_map/squeeze | solution.py:587
